TPU v7x, 32 devices: a whole 2x2x4 slice. The times are simulated.
32 devices in a mesh: dp: 16 (over z, y, core), own: 2 (over x).
Axes of the slice: x: 2, y: 2, z: 4, core: 2. Of those that a mesh axis runs over, the one named last changes fastest.
Arguments:
- layer_inputs: bfloat16 [4, 16, 16, 128, 128], P(None, 'dp', 'own'), as said below
- weights: bfloat16 [4, 1152, 128], replicated, may hold values from -0.1875 to 0.1875
- top_cotangent: bfloat16 [16, 16, 128, 128], P('dp', 'own'), may hold values from -6 to 6
- segmentation: int32 [16, 16, 128], P('dp', 'own'), may hold values from 0 to 2
- layer_slots: int32 [4], replicated, may hold values from 0 to 3, as said below
- a_inverse: bfloat16 [4, 1152, 1152], P('own', 'dp'), as said below
- g_inverse: bfloat16 [4, 128, 128], P('own'), as said below
Outputs:
- preconditioned: float32 [4, 1152, 128], P(None, 'dp')
- input_grad: bfloat16 [16, 16, 128, 128], P('dp', 'own')
Inputs may be any that keep to these rules, and one draw needn't show every extreme that they name: Distinct slot numbers; layer l is held by owner layer_slots[l] // 2, in that owner's slot layer_slots[l] % 2. One owner holds exactly 2 layers in every draw. `a_inverse`: each factor is symmetric. `g_inverse`: each factor is symmetric. `layer_inputs`: activations after a rectifier.
All inputs are finite; a program needn't handle non-finite values.
Results may differ from a plain program's by a relative error of at most 0.011.
Values may be sent and summed in bfloat16 or wider, within the bound.
A program may use at most 64 MiB of HBM per device.

v0:
```python
import math
import jax
import jax.numpy as jnp
from jax import lax
from jax.sharding import PartitionSpec as P


def extended(cells, sides, width):
    for axis, dim in sides:
        count = lax.axis_size(axis)
        ends = count - 1
        head = lax.slice_in_dim(cells, 0, width, axis=dim)
        tail = lax.slice_in_dim(cells, cells.shape[dim] - width, cells.shape[dim], axis=dim)
        cells = jnp.concatenate(
            [
                lax.ppermute(tail, axis, [(i, (i + 1) % count) for i in range(ends)]),
                cells,
                lax.ppermute(head, axis, [((i + 1) % count, i) for i in range(ends)]),
            ],
            axis=dim,
        )
    return cells


def from_root(block, axis, owner):
    block = jnp.where(lax.axis_index(axis) == owner, block, jnp.zeros_like(block))
    return lax.psum(block, axis)


def loss_weight(labels):
    return jnp.where(labels == 0, 1.0, jnp.where(labels == 1, 0.0, 0.5)).astype(jnp.float32)


def tap_matrix(padded, num_rows, num_cols):
    channels = padded.shape[-1]
    pieces = []
    for tap_index in range(9):
        row_start = 2 - tap_index // 3
        col_start = 2 - tap_index % 3
        pieces.append(padded[row_start : row_start + num_rows, col_start : col_start + num_cols])
    stacked = jnp.stack(pieces, axis=2)
    return stacked.reshape(num_rows * num_cols, 9 * channels)


def per_device(
    layer_inputs, weights, top_cotangent, segmentation, layer_slots, a_inverse, g_inverse
):
    layer_count = layer_inputs.shape[0]
    num_rows = layer_inputs.shape[2]
    num_cols = layer_inputs.shape[3]
    channels = layer_inputs.shape[4]
    data_devices = lax.axis_size("dp")
    owner_devices = lax.axis_size("own")
    grad_scale = 1.0 / math.sqrt(data_devices * owner_devices * num_rows * num_cols)
    inputs_local = layer_inputs[:, 0]
    scaled = loss_weight(segmentation[0])[:, :, None] * top_cotangent[0].astype(jnp.float32)
    out_grad = scaled.astype(jnp.bfloat16)
    grad_blocks = [None] * layer_count
    input_grad = None
    for layer_index in range(layer_count - 1, -1, -1):
        rimmed = extended(out_grad, (("own", 0),), 1)
        padded = jnp.pad(rimmed, ((0, 0), (1, 1), (0, 0)))
        tap_rows = tap_matrix(padded, num_rows, num_cols)
        flat_inputs = inputs_local[layer_index].reshape(num_rows * num_cols, channels)
        grad_block = lax.dot_general(
            flat_inputs, tap_rows, (((0,), (0,)), ((), ())), preferred_element_type=jnp.float32
        )
        grad_blocks[layer_index] = grad_block.reshape(9 * channels, channels) * grad_scale
        kernel = weights[layer_index].reshape(channels, 9 * channels)
        input_side = lax.dot_general(
            tap_rows, kernel, (((1,), (1,)), ((), ())), preferred_element_type=jnp.float32
        )
        input_side = input_side.reshape(num_rows, num_cols, channels)
        if layer_index > 0:
            out_grad = jnp.where(inputs_local[layer_index] > 0, input_side, 0.0).astype(
                jnp.bfloat16
            )
        else:
            input_grad = input_side.astype(jnp.bfloat16)[None]
    grad_term = jnp.concatenate(grad_blocks, axis=1)
    grad_rows = lax.psum_scatter(grad_term, "dp", scatter_dimension=0, tiled=True)
    slot_count = a_inverse.shape[0]
    grad_sum = lax.psum(grad_rows.astype(jnp.bfloat16), "own")
    left_panels = []
    right_panels = []
    for layer_index in range(layer_count):
        slot_id = layer_slots[layer_index]
        owner_index = slot_id // slot_count
        local_slot = slot_id % slot_count
        left_panel = lax.dynamic_index_in_dim(a_inverse, local_slot, 0, keepdims=False)
        right_panel = lax.dynamic_index_in_dim(g_inverse, local_slot, 0, keepdims=False)
        left_panel, right_panel = (
            from_root(left_panel, "own", owner_index),
            from_root(right_panel, "own", owner_index),
        )
        left_panels.append(left_panel)
        right_panels.append(right_panel)
    left_stack = jnp.stack(left_panels, axis=0)
    right_stack = jnp.stack(right_panels, axis=0)
    gathered_piece = lax.all_gather(grad_sum, "dp", axis=0, tiled=True)
    width_here = gathered_piece.shape[0]
    shaped_piece = gathered_piece.reshape(width_here, layer_count, channels)
    left_product = jnp.einsum(
        "lrn,nlc->lrc", left_stack, shaped_piece, preferred_element_type=jnp.float32
    )
    preconditioned = jnp.einsum(
        "lrc,lcd->lrd",
        left_product.astype(jnp.bfloat16),
        right_stack,
        preferred_element_type=jnp.float32,
    )
    return (preconditioned, input_grad)


def solution(mesh):
    in_specs = (
        P(None, "dp", "own", None, None),
        P(),
        P("dp", "own", None, None),
        P("dp", "own", None),
        P(),
        P("own", "dp", None),
        P("own", None, None),
    )
    out_specs = (P(None, "dp", None), P("dp", "own", None, None))
    return jax.shard_map(
        per_device, mesh=mesh, in_specs=in_specs, out_specs=out_specs, check_vma=False
    )
```

profile of v0, /device:TPU:0, one launch (start us, length us, event | category | flops | bytes accessed | tf_op | source)
XLA Modules:
  0.0 266.4 jit_solution(8736624988374941266)
XLA Ops:
  7.2 1.2 copy.10
  8.4 0.7 select_bitcast_fusion
  9.2 1.3 collective-permute-start.1
  10.5 4.8 %collective-permute-start = (bf16[1,128,128]{1,2,0:T(8,128)(2,1)S(1)}, bf16[1,128,128]{1,2,0:T(8,128)(2,1)S(1)}, u32[]{:S(2)}, u32[]{:S(2)}) collective-permute-start(bf16[1,128,128]{1,2,0:T(8,128)(2,1)S(1)} %get-tuple-element.29), channel_id=1, source_target_pairs={{0,1},{2,3},{4,5},{6,7},{8,9},{10,11},{12,13},{14,15},{16,17},{18,... | collective-permute-start | bytes 98312 | tf_op jit(solution)/shard_map/ppermute | solution.py:16
  15.4 1.3 fusion.111
  16.7 1.0 fusion.112
  17.7 0.4 reshape.134
  18.0 1.1 reshape.135
  19.1 1.1 reshape.136
  20.2 0.3 fusion.45
  20.5 0.1 fusion.101
  20.8 0.2 fusion.97
  21.2 0.2 fusion.95
  21.5 1.6 copy.30
  23.1 1.8 fusion.13
  25.0 0.6 fusion.115
  25.6 1.3 collective-permute-start.3
  26.9 5.1 %collective-permute-start.2 = (bf16[1,128,128]{2,1,0:T(8,128)(2,1)}, bf16[1,128,128]{2,1,0:T(8,128)(2,1)S(1)}, u32[]{:S(2)}, u32[]{:S(2)}) collective-permute-start(bf16[1,128,128]{2,1,0:T(8,128)(2,1)} %get-tuple-element.27), channel_id=1, source_target_pairs={{0,1},{2,3},{4,5},{6,7},{8,9},{10,11},{12,13},{14,15},{16,17},{18,... | collective-permute-start | bytes 98312 | tf_op jit(solution)/shard_map/ppermute | solution.py:16
  32.0 0.8 fusion.3
  32.8 0.2 copy.31
  33.1 0.8 collective-permute-done.2
  33.9 0.9 fusion.59
  34.9 0.8 fusion.90
  35.9 0.1 fusion.85
  36.1 2.7 copy.28
  38.8 2.5 copy.20
  41.2 2.7 %fusion.14 = bf16[8,128,128]{2,1,0:T(8,128)(2,1)S(1)} fusion(bf16[8,128,1152]{1,2,0:T(8,128)(2,1)} %bitcast.255, bf16[128,1152,1]{1,0,2:T(8,128)(2,1)} %reshape.135, bf16[4,1,8,128,128]{4,3,2,1,0:T(8,128)(2,1)} %param.7), kind=kOutput, calls=%fused_computation.24 | convolution fusion | flops 302383104 | bytes 3178496 | tf_op jit(solution)/shard_map/dot_general | solution.py:70
  44.0 0.6 fusion.114
  44.6 1.3 collective-permute-start.5
  45.9 5.3 %collective-permute-start.4 = (bf16[1,128,128]{2,1,0:T(8,128)(2,1)}, bf16[1,128,128]{2,1,0:T(8,128)(2,1)S(1)}, u32[]{:S(2)}, u32[]{:S(2)}) collective-permute-start(bf16[1,128,128]{2,1,0:T(8,128)(2,1)} %get-tuple-element.25), channel_id=1, source_target_pairs={{0,1},{2,3},{4,5},{6,7},{8,9},{10,11},{12,13},{14,15},{16,17},{18,... | collective-permute-start | bytes 98312 | tf_op jit(solution)/shard_map/ppermute | solution.py:16
  51.2 1.6 fusion.2
  52.8 1.3 copy.29
  54.1 0.9 mul.65
  55.0 0.9 fusion.57
  56.0 0.8 fusion.80
  57.2 2.7 copy.26
  59.9 2.5 copy.22
  62.3 2.7 %fusion.15 = bf16[8,128,128]{2,1,0:T(8,128)(2,1)S(1)} fusion(bf16[8,128,1152]{1,2,0:T(8,128)(2,1)} %bitcast.256, bf16[128,1152,1]{1,0,2:T(8,128)(2,1)} %reshape.136, bf16[4,1,8,128,128]{4,3,2,1,0:T(8,128)(2,1)} %param.7), kind=kOutput, calls=%fused_computation.25 | convolution fusion | flops 302383104 | bytes 3178496 | tf_op jit(solution)/shard_map/dot_general | solution.py:70
  65.1 0.6 fusion.113
  65.7 1.3 collective-permute-start.7
  67.0 5.1 %collective-permute-start.6 = (bf16[1,128,128]{2,1,0:T(8,128)(2,1)}, bf16[1,128,128]{2,1,0:T(8,128)(2,1)S(1)}, u32[]{:S(2)}, u32[]{:S(2)}) collective-permute-start(bf16[1,128,128]{2,1,0:T(8,128)(2,1)} %get-tuple-element.23), channel_id=1, source_target_pairs={{0,1},{2,3},{4,5},{6,7},{8,9},{10,11},{12,13},{14,15},{16,17},{18,... | collective-permute-start | bytes 98312 | tf_op jit(solution)/shard_map/ppermute | solution.py:16
  72.2 1.6 fusion.1
  73.7 1.3 copy.27
  75.0 0.9 mul.62
  75.9 0.9 select_maximum_fusion
  76.8 0.8 fusion.70
  78.1 2.7 copy.24
  80.8 3.3 %fusion = f32[128,1152]{0,1:T(8,128)} fusion(bf16[1024,128]{1,0:T(8,128)(2,1)S(1)} %bitcast.258, bf16[144,8,8,128]{3,2,1,0:T(8,128)(2,1)} %bitcast.257), kind=kOutput, calls=%fused_computation.4 | convolution fusion | flops 302137344 | bytes 3211264 | tf_op jit(solution)/shard_map/dot_general | solution.py:65
  84.0 2.1 copy.25
  86.2 1.9 mul.59
  88.1 3.0 %pad_maximum_fusion = f32[1152,512]{1,0:T(8,128)} fusion(f32[1152,128]{1,0:T(8,128)S(1)} %mul.68, f32[1152,128]{1,0:T(8,128)} %mul.65, f32[1152,128]{1,0:T(8,128)} %mul.62, f32[1152,128]{1,0:T(8,128)} %mul.59), kind=kLoop, calls=%fused_computation.16 | loop fusion | flops 1769472 | bytes 4718592 | tf_op jit(solution)/shard_map/concatenate | solution.py:80
  91.2 0.6 copy-done.9
  91.7 0.6 fusion.117
  102.6 0.9 dynamic-slice_select_fusion.3
  103.5 52.2 %reduce-scatter.2.cloned.1.call-done = f32[72,512]{1,0:T(8,128)} async-done(((f32[1152,512]{1,0:T(8,128)}), f32[72,512]{1,0:T(8,128)}) %reduce-scatter.2.cloned.1.call-update) | async-done | bytes 147472 | tf_op jit(solution)/shard_map/reduce_scatter | solution.py:81
  155.7 1.6 convert_element_type.58
  157.3 0.7 dynamic-slice_select_fusion.7
  158.1 34.0 %all-reduce.11.cloned.1.call-done = (bf16[72,512]{1,0:T(8,128)(2,1)}, bf16[1,72,1152]{2,1,0:T(8,128)(2,1)}, bf16[1,72,1152]{2,1,0:T(8,128)(2,1)}, bf16[1,72,1152]{2,1,0:T(8,128)(2,1)}, bf16[1,72,1152]{2,1,0:T(8,128)(2,1)}) async-done(((bf16[72,512]{1,0:T(8,128)(2,1)}, bf16[1,72,1152]{2,1,0:T(8,128)(2,1)}, bf16[1,72,1152]{2,1,0:T(8,128)(2,1)}, bf16[1,72,1152]{2,1,0:T(8,128)(2,1)}, ...) | async-done | bytes 737296 | tf_op jit(solution)/shard_map/psum | solution.py:83
  192.0 0.4 reshape.137
  192.4 2.5 copy.32
  194.9 3.3 %fusion.19 = bf16[1,8,128,128]{3,2,1,0:T(8,128)(2,1)} fusion(bf16[8,128,1152]{1,2,0:T(8,128)(2,1)} %bitcast.250, bf16[128,1152,1]{1,0,2:T(8,128)(2,1)S(1)} %reshape.137), kind=kOutput, calls=%fused_computation.30 | convolution fusion | flops 302120960 | bytes 2916352 | tf_op jit(solution)/shard_map/dot_general | solution.py:70
  198.2 18.3 %all-reduce.9.cloned.1.call-done = (bf16[1,128,128]{2,1,0:T(8,128)(2,1)}, bf16[1,128,128]{2,1,0:T(8,128)(2,1)}, bf16[1,128,128]{2,1,0:T(8,128)(2,1)}, bf16[1,128,128]{2,1,0:T(8,128)(2,1)}) async-done(((bf16[1,128,128]{2,1,0:T(8,128)(2,1)}, bf16[1,128,128]{2,1,0:T(8,128)(2,1)}, bf16[1,128,128]{2,1,0:T(8,128)(2,1)}, bf16[1,128,128]{2,1,0:T(8,128)(2,1)}), (bf16[1,128,128]{2,1,0:T(8,128)(2,1)}, ...) | async-done | bytes 131088 | tf_op jit(solution)/shard_map/psum | solution.py:27
  216.5 40.8 %all-gather.2.cloned.1.call-done = bf16[1152,512]{1,0:T(8,128)(2,1)} async-done(((bf16[72,512]{1,0:T(8,128)(2,1)}), bf16[1152,512]{1,0:T(8,128)(2,1)}) %all-gather.2.cloned.1.call-update) | async-done | bytes 1179664 | tf_op jit(solution)/shard_map/all_gather | solution.py:100
  257.3 2.5 fusion.24
  (74 shorter events, 2.1 us)
Async XLA Ops:
  7.2 9.5 %copy-start.3 = (bf16[4,1,8,128,128]{4,3,2,1,0:T(8,128)(2,1)S(1)}, bf16[4,1,8,128,128]{4,3,2,1,0:T(8,128)(2,1)}, u32[]{:S(2)}) copy-start(bf16[4,1,8,128,128]{4,3,2,1,0:T(8,128)(2,1)} %param.7) | copy-start | bytes 3145732
  7.2 148.5 %reduce-scatter.2.cloned.1.call-start = ((), (), s32[]{:S(2)}) async-start(), calls=%async_computation.1 | async-start | bytes 2506752 | tf_op jit(solution)/shard_map/reduce_scatter | solution.py:81
  9.2 11.0 %collective-permute-start.1 = (bf16[1,128,128]{1,2,0:T(8,128)(2,1)S(1)}, bf16[1,128,128]{1,2,0:T(8,128)(2,1)S(1)}, u32[]{:S(2)}, u32[]{:S(2)}) collective-permute-start(bf16[1,128,128]{1,2,0:T(8,128)(2,1)S(1)} %get-tuple-element.30), channel_id=1, source_target_pairs={{1,0},{3,2},{5,4},{7,6},{9,8},{11,10},{13,12},{15,14},{17,16},{19,... | collective-permute-start | bytes 98312 | tf_op jit(solution)/shard_map/ppermute | solution.py:18
  10.5 9.7 %collective-permute-start = (bf16[1,128,128]{1,2,0:T(8,128)(2,1)S(1)}, bf16[1,128,128]{1,2,0:T(8,128)(2,1)S(1)}, u32[]{:S(2)}, u32[]{:S(2)}) collective-permute-start(bf16[1,128,128]{1,2,0:T(8,128)(2,1)S(1)} %get-tuple-element.29), channel_id=1, source_target_pairs={{0,1},{2,3},{4,5},{6,7},{8,9},{10,11},{12,13},{14,15},{16,17},{18,... | collective-permute-start | bytes 98312 | tf_op jit(solution)/shard_map/ppermute | solution.py:16
  23.1 8.9 %copy-start.8 = (bf16[1,1,8,128,128]{4,3,2,1,0:T(8,128)(2,1)S(1)}, bf16[1,1,8,128,128]{4,3,2,1,0:T(8,128)(2,1)}, u32[]{:S(2)}) copy-start(bf16[1,1,8,128,128]{4,3,2,1,0:T(8,128)(2,1)} %get-tuple-element.18) | copy-start | bytes 786436
  25.6 7.5 %collective-permute-start.3 = (bf16[1,128,128]{2,1,0:T(8,128)(2,1)}, bf16[1,128,128]{2,1,0:T(8,128)(2,1)}, u32[]{:S(2)}, u32[]{:S(2)}) collective-permute-start(bf16[1,128,128]{2,1,0:T(8,128)(2,1)} %get-tuple-element.28), channel_id=1, source_target_pairs={{1,0},{3,2},{5,4},{7,6},{9,8},{11,10},{13,12},{15,14},{17,16},{19,... | collective-permute-start | bytes 98312 | tf_op jit(solution)/shard_map/ppermute | solution.py:18
  26.9 7.0 %collective-permute-start.2 = (bf16[1,128,128]{2,1,0:T(8,128)(2,1)}, bf16[1,128,128]{2,1,0:T(8,128)(2,1)S(1)}, u32[]{:S(2)}, u32[]{:S(2)}) collective-permute-start(bf16[1,128,128]{2,1,0:T(8,128)(2,1)} %get-tuple-element.27), channel_id=1, source_target_pairs={{0,1},{2,3},{4,5},{6,7},{8,9},{10,11},{12,13},{14,15},{16,17},{18,... | collective-permute-start | bytes 98312 | tf_op jit(solution)/shard_map/ppermute | solution.py:16
  41.2 10.0 %copy-start = (bf16[8,128,9,128]{1,0,3,2:T(8,128)(2,1)S(1)}, bf16[8,128,9,128]{1,0,3,2:T(8,128)(2,1)}, u32[]{:S(2)}) copy-start(bf16[8,128,9,128]{1,0,3,2:T(8,128)(2,1)} %copy.28) | copy-start | bytes 7077892
  41.2 10.0 %copy-start.7 = (bf16[1,1,8,128,128]{4,3,2,1,0:T(8,128)(2,1)S(1)}, bf16[1,1,8,128,128]{4,3,2,1,0:T(8,128)(2,1)}, u32[]{:S(2)}) copy-start(bf16[1,1,8,128,128]{4,3,2,1,0:T(8,128)(2,1)} %get-tuple-element.16) | copy-start | bytes 786436
  44.6 10.4 %collective-permute-start.5 = (bf16[1,128,128]{2,1,0:T(8,128)(2,1)}, bf16[1,128,128]{2,1,0:T(8,128)(2,1)}, u32[]{:S(2)}, u32[]{:S(2)}) collective-permute-start(bf16[1,128,128]{2,1,0:T(8,128)(2,1)} %get-tuple-element.26), channel_id=1, source_target_pairs={{1,0},{3,2},{5,4},{7,6},{9,8},{11,10},{13,12},{15,14},{17,16},{19,... | collective-permute-start | bytes 98312 | tf_op jit(solution)/shard_map/ppermute | solution.py:18
  45.9 9.1 %collective-permute-start.4 = (bf16[1,128,128]{2,1,0:T(8,128)(2,1)}, bf16[1,128,128]{2,1,0:T(8,128)(2,1)S(1)}, u32[]{:S(2)}, u32[]{:S(2)}) collective-permute-start(bf16[1,128,128]{2,1,0:T(8,128)(2,1)} %get-tuple-element.25), channel_id=1, source_target_pairs={{0,1},{2,3},{4,5},{6,7},{8,9},{10,11},{12,13},{14,15},{16,17},{18,... | collective-permute-start | bytes 98312 | tf_op jit(solution)/shard_map/ppermute | solution.py:16
  62.3 9.8 %copy-start.1 = (bf16[8,128,9,128]{1,0,3,2:T(8,128)(2,1)S(1)}, bf16[8,128,9,128]{1,0,3,2:T(8,128)(2,1)}, u32[]{:S(2)}) copy-start(bf16[8,128,9,128]{1,0,3,2:T(8,128)(2,1)} %copy.26) | copy-start | bytes 7077892
  62.3 9.8 %copy-start.6 = (bf16[1,1,8,128,128]{4,3,2,1,0:T(8,128)(2,1)S(1)}, bf16[1,1,8,128,128]{4,3,2,1,0:T(8,128)(2,1)}, u32[]{:S(2)}) copy-start(bf16[1,1,8,128,128]{4,3,2,1,0:T(8,128)(2,1)} %get-tuple-element.17) | copy-start | bytes 786436
  65.7 10.2 %collective-permute-start.7 = (bf16[1,128,128]{2,1,0:T(8,128)(2,1)}, bf16[1,128,128]{2,1,0:T(8,128)(2,1)}, u32[]{:S(2)}, u32[]{:S(2)}) collective-permute-start(bf16[1,128,128]{2,1,0:T(8,128)(2,1)} %get-tuple-element.24), channel_id=1, source_target_pairs={{1,0},{3,2},{5,4},{7,6},{9,8},{11,10},{13,12},{15,14},{17,16},{19,... | collective-permute-start | bytes 98312 | tf_op jit(solution)/shard_map/ppermute | solution.py:18
  67.0 8.9 %collective-permute-start.6 = (bf16[1,128,128]{2,1,0:T(8,128)(2,1)}, bf16[1,128,128]{2,1,0:T(8,128)(2,1)S(1)}, u32[]{:S(2)}, u32[]{:S(2)}) collective-permute-start(bf16[1,128,128]{2,1,0:T(8,128)(2,1)} %get-tuple-element.23), channel_id=1, source_target_pairs={{0,1},{2,3},{4,5},{6,7},{8,9},{10,11},{12,13},{14,15},{16,17},{18,... | collective-permute-start | bytes 98312 | tf_op jit(solution)/shard_map/ppermute | solution.py:16
  78.1 2.7 %copy-start.5 = (bf16[1,1,8,128,128]{4,3,2,1,0:T(8,128)(2,1)S(1)}, bf16[1,1,8,128,128]{4,3,2,1,0:T(8,128)(2,1)}, u32[]{:S(2)}) copy-start(bf16[1,1,8,128,128]{4,3,2,1,0:T(8,128)(2,1)} %get-tuple-element.15) | copy-start | bytes 786436
  91.1 0.7 copy-start.9
  91.1 11.6 %copy-start.2 = (bf16[2,72,1152]{2,1,0:T(8,128)(2,1)S(1)}, bf16[2,72,1152]{2,1,0:T(8,128)(2,1)}, u32[]{:S(2)}) copy-start(bf16[2,72,1152]{2,1,0:T(8,128)(2,1)} %param.12) | copy-start | bytes 995332
  91.1 66.2 %copy-start.4 = (bf16[2,128,128]{2,1,0:T(8,128)(2,1)S(1)}, bf16[2,128,128]{2,1,0:T(8,128)(2,1)}, u32[]{:S(2)}) copy-start(bf16[2,128,128]{2,1,0:T(8,128)(2,1)} %param.13) | copy-start | bytes 196612
  91.1 100.9 %all-reduce.11.cloned.1.call-start = ((), (), s32[]{:S(2)}) async-start(), calls=%async_computation.4 | async-start | bytes 1474560 | tf_op jit(solution)/shard_map/psum | solution.py:83
  157.3 59.2 %all-reduce.9.cloned.1.call-start = ((), (), s32[]{:S(2)}) async-start(), calls=%async_computation.3 | async-start | bytes 262144 | tf_op jit(solution)/shard_map/psum | solution.py:27
  158.0 99.3 %all-gather.2.cloned.1.call-start = ((), (), s32[]{:S(2)}) async-start(), calls=%async_computation.2 | async-start | bytes 1253376 | tf_op jit(solution)/shard_map/all_gather | solution.py:100
  194.9 62.4 %copy-start.10 = (bf16[1,72,1152]{2,1,0:T(8,128)(2,1)S(1)}, bf16[1,72,1152]{2,1,0:T(8,128)(2,1)}, u32[]{:S(2)}) copy-start(bf16[1,72,1152]{2,1,0:T(8,128)(2,1)} %get-tuple-element.7) | copy-start | bytes 497668
  194.9 62.4 %copy-start.11 = (bf16[1,72,1152]{2,1,0:T(8,128)(2,1)S(1)}, bf16[1,72,1152]{2,1,0:T(8,128)(2,1)}, u32[]{:S(2)}) copy-start(bf16[1,72,1152]{2,1,0:T(8,128)(2,1)} %get-tuple-element.8) | copy-start | bytes 497668
  194.9 62.4 %copy-start.12 = (bf16[1,72,1152]{2,1,0:T(8,128)(2,1)S(1)}, bf16[1,72,1152]{2,1,0:T(8,128)(2,1)}, u32[]{:S(2)}) copy-start(bf16[1,72,1152]{2,1,0:T(8,128)(2,1)} %get-tuple-element.9) | copy-start | bytes 497668
  194.9 62.4 %copy-start.13 = (bf16[1,72,1152]{2,1,0:T(8,128)(2,1)S(1)}, bf16[1,72,1152]{2,1,0:T(8,128)(2,1)}, u32[]{:S(2)}) copy-start(bf16[1,72,1152]{2,1,0:T(8,128)(2,1)} %get-tuple-element.10) | copy-start | bytes 497668
Sparse Core Ops, SparseCore 0:
  91.2 64.3 reduce-scatter.1
  159.0 32.9 all-reduce.10
  194.6 21.8 all-reduce.8
  218.9 38.3 all-gather.1
where the time goes:
time: 268 us; the launch traced here: 266 us
  waiting for transfers between devices  146 us (54%)
  local copies, waits for them, and re-layouts  37.2 us (14%)
  starting transfers between devices  25.7 us (10%)
  between operations  24.6 us (9%)
  matrix products  20.3 us (8%)
  other arithmetic  12.4 us (5%)
    reduce_scatter x1, waiting for transfers between devices, per_device(): lax.psum_scatter(grad_term, 'dp', scatter_dimension=0, tiled=True)  52.2 us
    all_gather x1, waiting for transfers between devices, per_device(): gathered_piece = lax.all_gather(grad_sum, 'dp', axis=0, tiled=True)  40.8 us
    psum x1, waiting for transfers between devices, per_device(): grad_sum = lax.psum(grad_rows.astype(jnp.bfloat16), 'own')  34 us
    ppermute x4, starting transfers between devices, extended(): lax.ppermute(tail, axis, [(i, (i + 1) % count) for i in range(ends)])  20.4 us
    psum x1, waiting for transfers between devices, from_root(): return lax.psum(block, axis)  18.3 us
    another operation x11, local copies, waits for them, and re-layouts, tap_matrix(): stacked = jnp.stack(pieces, axis=2)  17.2 us
    dot_general x4, matrix products, per_device(): lax.dot_general(tap_rows, kernel, (((1,), (1,)), ((), ())), preferred_ele...  10.5 us
    mul x8, local copies, waits for them, and re-layouts, per_device(): grad_block.reshape(9 * channels, channels) * grad_scale  8.66 us
  transfers between devices with their start and end apart: 12, of which 5 were waited for; matrix products, arithmetic and copies ran while one was open for 8% of the time, Pallas kernels for 0%

commit v1 on v0

--- a/solution.py
+++ b/solution.py
@@ -3,6 +3,8 @@
 import jax.numpy as jnp
 from jax import lax
 from jax.sharding import PartitionSpec as P
+
+draft_floor_all = lambda target, across: jnp.sum(lax.all_gather(target, across), 0)
 
 
 def extended(cells, sides, width):
@@ -24,7 +26,7 @@
 
 def from_root(block, axis, owner):
     block = jnp.where(lax.axis_index(axis) == owner, block, jnp.zeros_like(block))
-    return lax.psum(block, axis)
+    return draft_floor_all(block, axis)
 
 
 def loss_weight(labels):

time: 268 us -> 253 us (0.944)
  waiting for transfers between devices: 146 us -> 86.4 us
  blocking collectives: 0 us -> 42.8 us
    all_gather x0 -> x8, blocking collectives: none -> 42.8 us  [lax.all_gather(target, across)]
    all_gather x1, waiting for transfers between devices: 40.8 us -> 0.01 us  [per_device(): gathered_piece = lax.all_gather(grad_sum, 'dp', axis=0, tiled=True)]
    psum x1 -> x0, waiting for transfers between devices: 18.3 us -> none  [from_root(): return lax.psum(block, axis)]
    psum x1, waiting for transfers between devices: 34 us -> 21 us  [per_device(): grad_sum = lax.psum(grad_rows.astype(jnp.bfloat16), 'own')]
    reduce_scatter x1, waiting for transfers between devices: 52.2 us -> 64.5 us  [per_device(): lax.psum_scatter(grad_term, 'dp', scatter_dimension=0, tiled=True)]
  transfers between devices with their start and end apart: 12 -> 11, of which waited for: 5 -> 3; matrix products, arithmetic and copies ran while one was open for 8% -> 9% of each run, Pallas kernels for 0% -> 0%
where the time goes in v1:
time: 253 us; the launch traced here: 251 us
  waiting for transfers between devices  86.4 us (34%)
  blocking collectives  42.8 us (17%)
  local copies, waits for them, and re-layouts  38.3 us (15%)
  starting transfers between devices  25.7 us (10%)
  between operations  24.9 us (10%)
  matrix products  19.1 us (8%)
  other arithmetic  14 us (6%)
    reduce_scatter x1, waiting for transfers between devices, per_device(): lax.psum_scatter(grad_term, 'dp', scatter_dimension=0, tiled=True)  64.5 us
    all_gather x8, blocking collectives, lax.all_gather(target, across)  42.8 us
    psum x1, waiting for transfers between devices, per_device(): grad_sum = lax.psum(grad_rows.astype(jnp.bfloat16), 'own')  21 us
    ppermute x4, starting transfers between devices, extended(): lax.ppermute(tail, axis, [(i, (i + 1) % count) for i in range(ends)])  20.5 us
    another operation x11, local copies, waits for them, and re-layouts, tap_matrix(): stacked = jnp.stack(pieces, axis=2)  17.2 us
    dot_general x4, matrix products, per_device(): lax.dot_general(tap_rows, kernel, (((1,), (1,)), ((), ())), preferred_ele...  10.5 us
    mul x8, local copies, waits for them, and re-layouts, per_device(): grad_block.reshape(9 * channels, channels) * grad_scale  8.63 us
    dot_general x4, matrix products, per_device(): lax.dot_general(flat_inputs, tap_rows, (((0,), (0,)), ((), ())), preferre...  7.25 us
  transfers between devices with their start and end apart: 11, of which 3 were waited for; matrix products, arithmetic and copies ran while one was open for 9% of the time, Pallas kernels for 0%

profile of v1, /device:TPU:0, one launch (start us, length us, event | category | flops | bytes accessed | tf_op | source)
XLA Modules:
  0.0 251.3 jit_solution(16034031647148668245)
XLA Ops:
  7.2 1.2 copy.58
  8.4 0.7 select_bitcast_fusion
  9.2 1.3 collective-permute-start.1
  10.5 4.8 %collective-permute-start = (bf16[1,128,128]{1,2,0:T(8,128)(2,1)S(1)}, bf16[1,128,128]{1,2,0:T(8,128)(2,1)S(1)}, u32[]{:S(2)}, u32[]{:S(2)}) collective-permute-start(bf16[1,128,128]{1,2,0:T(8,128)(2,1)S(1)} %get-tuple-element.20), channel_id=1, source_target_pairs={{0,1},{2,3},{4,5},{6,7},{8,9},{10,11},{12,13},{14,15},{16,17},{18,... | collective-permute-start | bytes 98312 | tf_op jit(solution)/shard_map/ppermute | solution.py:18
  15.4 1.3 fusion.103
  16.7 1.0 fusion.104
  18.0 1.1 reshape.103
  19.1 1.1 reshape.104
  21.5 1.6 copy.78
  23.1 1.8 fusion.13
  25.0 0.6 fusion.107
  25.6 1.3 collective-permute-start.3
  26.9 5.1 %collective-permute-start.2 = (bf16[1,128,128]{2,1,0:T(8,128)(2,1)}, bf16[1,128,128]{2,1,0:T(8,128)(2,1)S(1)}, u32[]{:S(2)}, u32[]{:S(2)}) collective-permute-start(bf16[1,128,128]{2,1,0:T(8,128)(2,1)} %get-tuple-element.18), channel_id=1, source_target_pairs={{0,1},{2,3},{4,5},{6,7},{8,9},{10,11},{12,13},{14,15},{16,17},{18,... | collective-permute-start | bytes 98312 | tf_op jit(solution)/shard_map/ppermute | solution.py:18
  32.0 0.8 fusion.3
  33.1 0.8 collective-permute-done.2
  33.9 0.9 fusion.51
  34.9 0.8 fusion.82
  36.1 2.6 %copy.76 = bf16[8,128,9,128]{1,0,3,2:T(8,128)(2,1)} copy(bf16[8,128,9,128]{3,1,0,2:T(8,128)(2,1)S(1)} %fusion.74) | data formatting | bytes 4718592 | tf_op jit(solution)/shard_map/stack | solution.py:43
  38.8 2.5 copy.68
  41.2 2.7 %fusion.14 = bf16[8,128,128]{2,1,0:T(8,128)(2,1)S(1)} fusion(bf16[8,128,1152]{1,2,0:T(8,128)(2,1)} %bitcast.253, bf16[128,1152,1]{1,0,2:T(8,128)(2,1)} %reshape.103, bf16[4,1,8,128,128]{4,3,2,1,0:T(8,128)(2,1)} %param.7), kind=kOutput, calls=%fused_computation.24 | convolution fusion | flops 302383104 | bytes 3178496 | tf_op jit(solution)/shard_map/dot_general | solution.py:72
  44.0 0.6 fusion.106
  44.6 1.3 collective-permute-start.5
  45.9 5.3 %collective-permute-start.4 = (bf16[1,128,128]{2,1,0:T(8,128)(2,1)}, bf16[1,128,128]{2,1,0:T(8,128)(2,1)S(1)}, u32[]{:S(2)}, u32[]{:S(2)}) collective-permute-start(bf16[1,128,128]{2,1,0:T(8,128)(2,1)} %get-tuple-element.16), channel_id=1, source_target_pairs={{0,1},{2,3},{4,5},{6,7},{8,9},{10,11},{12,13},{14,15},{16,17},{18,... | collective-permute-start | bytes 98312 | tf_op jit(solution)/shard_map/ppermute | solution.py:18
  51.2 1.6 fusion.2
  52.8 1.3 copy.77
  54.1 0.9 mul.65
  55.0 0.9 fusion.49
  56.0 0.8 fusion.72
  57.2 2.6 %copy.74 = bf16[8,128,9,128]{1,0,3,2:T(8,128)(2,1)} copy(bf16[8,128,9,128]{3,1,0,2:T(8,128)(2,1)S(1)} %fusion.64) | data formatting | bytes 4718592 | tf_op jit(solution)/shard_map/stack | solution.py:43
  59.9 2.5 copy.70
  62.4 2.7 %fusion.15 = bf16[8,128,128]{2,1,0:T(8,128)(2,1)S(1)} fusion(bf16[8,128,1152]{1,2,0:T(8,128)(2,1)} %bitcast.254, bf16[128,1152,1]{1,0,2:T(8,128)(2,1)} %reshape.104, bf16[4,1,8,128,128]{4,3,2,1,0:T(8,128)(2,1)} %param.7), kind=kOutput, calls=%fused_computation.25 | convolution fusion | flops 302383104 | bytes 3178496 | tf_op jit(solution)/shard_map/dot_general | solution.py:72
  65.1 0.6 fusion.105
  65.7 1.3 collective-permute-start.7
  67.0 5.1 %collective-permute-start.6 = (bf16[1,128,128]{2,1,0:T(8,128)(2,1)}, bf16[1,128,128]{2,1,0:T(8,128)(2,1)S(1)}, u32[]{:S(2)}, u32[]{:S(2)}) collective-permute-start(bf16[1,128,128]{2,1,0:T(8,128)(2,1)} %get-tuple-element.14), channel_id=1, source_target_pairs={{0,1},{2,3},{4,5},{6,7},{8,9},{10,11},{12,13},{14,15},{16,17},{18,... | collective-permute-start | bytes 98312 | tf_op jit(solution)/shard_map/ppermute | solution.py:18
  72.2 1.6 fusion.1
  73.8 1.3 copy.75
  75.1 0.9 mul.62
  75.9 0.9 select_maximum_fusion
  76.9 0.8 fusion.62
  78.2 2.6 %copy.72 = bf16[8,128,9,128]{1,0,3,2:T(8,128)(2,1)} copy(bf16[8,128,9,128]{3,1,0,2:T(8,128)(2,1)S(1)} %fusion.54) | data formatting | bytes 4718592 | tf_op jit(solution)/shard_map/stack | solution.py:43
  80.8 3.3 %fusion = f32[128,1152]{0,1:T(8,128)} fusion(bf16[1024,128]{1,0:T(8,128)(2,1)S(1)} %bitcast.257, bf16[144,8,8,128]{3,2,1,0:T(8,128)(2,1)} %bitcast.255), kind=kOutput, calls=%fused_computation.4 | convolution fusion | flops 302137344 | bytes 3211264 | tf_op jit(solution)/shard_map/dot_general | solution.py:67
  84.1 2.1 copy.73
  86.2 1.9 mul.59
  88.1 3.0 %pad_maximum_fusion = f32[1152,512]{1,0:T(8,128)} fusion(f32[1152,128]{1,0:T(8,128)S(1)} %mul.68, f32[1152,128]{1,0:T(8,128)} %mul.65, f32[1152,128]{1,0:T(8,128)} %mul.62, f32[1152,128]{1,0:T(8,128)} %mul.59), kind=kLoop, calls=%fused_computation.16 | loop fusion | flops 1769472 | bytes 4718592 | tf_op jit(solution)/shard_map/concatenate | solution.py:82
  91.2 64.5 %reduce-scatter.2.cloned.1.call-done = f32[72,512]{1,0:T(8,128)} async-done(((f32[1152,512]{1,0:T(8,128)}), f32[72,512]{1,0:T(8,128)}) %reduce-scatter.2.cloned.1.call-update) | async-done | bytes 147472 | tf_op jit(solution)/shard_map/reduce_scatter | solution.py:83
  155.7 1.6 convert_element_type.74
  157.3 21.0 %all-reduce.6.cloned.1.call-done = bf16[72,512]{1,0:T(8,128)(2,1)} async-done(((bf16[72,512]{1,0:T(8,128)(2,1)}), bf16[72,512]{1,0:T(8,128)(2,1)}) %all-reduce.6.cloned.1.call-update) | async-done | bytes 73744 | tf_op jit(solution)/shard_map/psum | solution.py:85
  178.4 0.7 fusion.109
  189.7 6.4 %all_gather.38 = bf16[2,72,1152]{2,1,0:T(8,128)(2,1)S(1)} all-gather(bf16[1,72,1152]{2,1,0:T(8,128)(2,1)S(1)} %get-tuple-element.12), channel_id=1, replica_groups=mesh['dp'=16,'own'=2] {'own'}, dimensions={0}, use_global_device_ids=true | all-gather | bytes 497664 | tf_op jit(solution)/shard_map/all_gather | solution.py:7
  196.1 0.7 reduce_sum.99
  196.8 6.0 %all_gather.37 = bf16[2,72,1152]{2,1,0:T(8,128)(2,1)S(1)} all-gather(bf16[1,72,1152]{2,1,0:T(8,128)(2,1)S(1)} %get-tuple-element.13), channel_id=1, replica_groups=mesh['dp'=16,'own'=2] {'own'}, dimensions={0}, use_global_device_ids=true | all-gather | bytes 497664 | tf_op jit(solution)/shard_map/all_gather | solution.py:7
  202.9 6.0 %all_gather.36 = bf16[2,72,1152]{2,1,0:T(8,128)(2,1)S(1)} all-gather(bf16[1,72,1152]{2,1,0:T(8,128)(2,1)S(1)} %get-tuple-element.11), channel_id=1, replica_groups=mesh['dp'=16,'own'=2] {'own'}, dimensions={0}, use_global_device_ids=true | all-gather | bytes 497664 | tf_op jit(solution)/shard_map/all_gather | solution.py:7
  209.0 6.0 %all_gather.35 = bf16[2,72,1152]{2,1,0:T(8,128)(2,1)S(1)} all-gather(bf16[1,72,1152]{2,1,0:T(8,128)(2,1)S(1)} %get-tuple-element.10), channel_id=1, replica_groups=mesh['dp'=16,'own'=2] {'own'}, dimensions={0}, use_global_device_ids=true | all-gather | bytes 497664 | tf_op jit(solution)/shard_map/all_gather | solution.py:7
  215.1 0.9 dynamic-slice_select_fusion.7
  216.0 4.6 %all_gather.43 = bf16[2,128,128]{2,1,0:T(8,128)(2,1)S(1)} all-gather(bf16[1,128,128]{2,1,0:T(8,128)(2,1)S(1)} %get-tuple-element.24), channel_id=1, replica_groups=mesh['dp'=16,'own'=2] {'own'}, dimensions={0}, use_global_device_ids=true | all-gather | bytes 98304 | tf_op jit(solution)/shard_map/all_gather | solution.py:7
  220.6 4.6 %all_gather.42 = bf16[2,128,128]{2,1,0:T(8,128)(2,1)S(1)} all-gather(bf16[1,128,128]{2,1,0:T(8,128)(2,1)S(1)} %get-tuple-element.25), channel_id=1, replica_groups=mesh['dp'=16,'own'=2] {'own'}, dimensions={0}, use_global_device_ids=true | all-gather | bytes 98304 | tf_op jit(solution)/shard_map/all_gather | solution.py:7
  225.2 4.6 %all_gather.41 = bf16[2,128,128]{2,1,0:T(8,128)(2,1)S(1)} all-gather(bf16[1,128,128]{2,1,0:T(8,128)(2,1)S(1)} %get-tuple-element.23), channel_id=1, replica_groups=mesh['dp'=16,'own'=2] {'own'}, dimensions={0}, use_global_device_ids=true | all-gather | bytes 98304 | tf_op jit(solution)/shard_map/all_gather | solution.py:7
  229.8 0.6 reduce_sum.101
  230.4 4.6 %all_gather.40 = bf16[2,128,128]{2,1,0:T(8,128)(2,1)S(1)} all-gather(bf16[1,128,128]{2,1,0:T(8,128)(2,1)S(1)} %get-tuple-element.22), channel_id=1, replica_groups=mesh['dp'=16,'own'=2] {'own'}, dimensions={0}, use_global_device_ids=true | all-gather | bytes 98304 | tf_op jit(solution)/shard_map/all_gather | solution.py:7
  235.0 0.6 reduce_sum.100
  236.0 2.5 copy.82
  238.4 3.2 %fusion.16 = bf16[1,8,128,128]{3,2,1,0:T(8,128)(2,1)} fusion(bf16[8,128,1152]{1,2,0:T(8,128)(2,1)} %bitcast.248, bf16[128,1152,1]{1,0,2:T(8,128)(2,1)S(1)} %reshape.105), kind=kOutput, calls=%fused_computation.27 | convolution fusion | flops 302120960 | bytes 2916352 | tf_op jit(solution)/shard_map/dot_general | solution.py:72
  241.7 1.7 copy.80
  243.4 1.4 fusion.17
  (84 shorter events, 4.2 us)
Async XLA Ops:
  7.2 9.5 %copy-start.3 = (bf16[4,1,8,128,128]{4,3,2,1,0:T(8,128)(2,1)S(1)}, bf16[4,1,8,128,128]{4,3,2,1,0:T(8,128)(2,1)}, u32[]{:S(2)}) copy-start(bf16[4,1,8,128,128]{4,3,2,1,0:T(8,128)(2,1)} %param.7) | copy-start | bytes 3145732
  7.2 148.5 %reduce-scatter.2.cloned.1.call-start = ((), (), s32[]{:S(2)}) async-start(), calls=%async_computation.1 | async-start | bytes 2506752 | tf_op jit(solution)/shard_map/reduce_scatter | solution.py:83
  9.2 11.0 %collective-permute-start.1 = (bf16[1,128,128]{1,2,0:T(8,128)(2,1)S(1)}, bf16[1,128,128]{1,2,0:T(8,128)(2,1)S(1)}, u32[]{:S(2)}, u32[]{:S(2)}) collective-permute-start(bf16[1,128,128]{1,2,0:T(8,128)(2,1)S(1)} %get-tuple-element.21), channel_id=1, source_target_pairs={{1,0},{3,2},{5,4},{7,6},{9,8},{11,10},{13,12},{15,14},{17,16},{19,... | collective-permute-start | bytes 98312 | tf_op jit(solution)/shard_map/ppermute | solution.py:20
  10.5 9.7 %collective-permute-start = (bf16[1,128,128]{1,2,0:T(8,128)(2,1)S(1)}, bf16[1,128,128]{1,2,0:T(8,128)(2,1)S(1)}, u32[]{:S(2)}, u32[]{:S(2)}) collective-permute-start(bf16[1,128,128]{1,2,0:T(8,128)(2,1)S(1)} %get-tuple-element.20), channel_id=1, source_target_pairs={{0,1},{2,3},{4,5},{6,7},{8,9},{10,11},{12,13},{14,15},{16,17},{18,... | collective-permute-start | bytes 98312 | tf_op jit(solution)/shard_map/ppermute | solution.py:18
  23.1 8.9 %copy-start.7 = (bf16[1,1,8,128,128]{4,3,2,1,0:T(8,128)(2,1)S(1)}, bf16[1,1,8,128,128]{4,3,2,1,0:T(8,128)(2,1)}, u32[]{:S(2)}) copy-start(bf16[1,1,8,128,128]{4,3,2,1,0:T(8,128)(2,1)} %get-tuple-element.9) | copy-start | bytes 786436
  25.6 7.5 %collective-permute-start.3 = (bf16[1,128,128]{2,1,0:T(8,128)(2,1)}, bf16[1,128,128]{2,1,0:T(8,128)(2,1)}, u32[]{:S(2)}, u32[]{:S(2)}) collective-permute-start(bf16[1,128,128]{2,1,0:T(8,128)(2,1)} %get-tuple-element.19), channel_id=1, source_target_pairs={{1,0},{3,2},{5,4},{7,6},{9,8},{11,10},{13,12},{15,14},{17,16},{19,... | collective-permute-start | bytes 98312 | tf_op jit(solution)/shard_map/ppermute | solution.py:20
  26.9 7.0 %collective-permute-start.2 = (bf16[1,128,128]{2,1,0:T(8,128)(2,1)}, bf16[1,128,128]{2,1,0:T(8,128)(2,1)S(1)}, u32[]{:S(2)}, u32[]{:S(2)}) collective-permute-start(bf16[1,128,128]{2,1,0:T(8,128)(2,1)} %get-tuple-element.18), channel_id=1, source_target_pairs={{0,1},{2,3},{4,5},{6,7},{8,9},{10,11},{12,13},{14,15},{16,17},{18,... | collective-permute-start | bytes 98312 | tf_op jit(solution)/shard_map/ppermute | solution.py:18
  41.2 10.0 %copy-start = (bf16[8,128,9,128]{1,0,3,2:T(8,128)(2,1)S(1)}, bf16[8,128,9,128]{1,0,3,2:T(8,128)(2,1)}, u32[]{:S(2)}) copy-start(bf16[8,128,9,128]{1,0,3,2:T(8,128)(2,1)} %copy.76) | copy-start | bytes 7077892
  41.2 10.0 %copy-start.6 = (bf16[1,1,8,128,128]{4,3,2,1,0:T(8,128)(2,1)S(1)}, bf16[1,1,8,128,128]{4,3,2,1,0:T(8,128)(2,1)}, u32[]{:S(2)}) copy-start(bf16[1,1,8,128,128]{4,3,2,1,0:T(8,128)(2,1)} %get-tuple-element.7) | copy-start | bytes 786436
  44.6 10.4 %collective-permute-start.5 = (bf16[1,128,128]{2,1,0:T(8,128)(2,1)}, bf16[1,128,128]{2,1,0:T(8,128)(2,1)}, u32[]{:S(2)}, u32[]{:S(2)}) collective-permute-start(bf16[1,128,128]{2,1,0:T(8,128)(2,1)} %get-tuple-element.17), channel_id=1, source_target_pairs={{1,0},{3,2},{5,4},{7,6},{9,8},{11,10},{13,12},{15,14},{17,16},{19,... | collective-permute-start | bytes 98312 | tf_op jit(solution)/shard_map/ppermute | solution.py:20
  45.9 9.1 %collective-permute-start.4 = (bf16[1,128,128]{2,1,0:T(8,128)(2,1)}, bf16[1,128,128]{2,1,0:T(8,128)(2,1)S(1)}, u32[]{:S(2)}, u32[]{:S(2)}) collective-permute-start(bf16[1,128,128]{2,1,0:T(8,128)(2,1)} %get-tuple-element.16), channel_id=1, source_target_pairs={{0,1},{2,3},{4,5},{6,7},{8,9},{10,11},{12,13},{14,15},{16,17},{18,... | collective-permute-start | bytes 98312 | tf_op jit(solution)/shard_map/ppermute | solution.py:18
  62.3 9.8 %copy-start.1 = (bf16[8,128,9,128]{1,0,3,2:T(8,128)(2,1)S(1)}, bf16[8,128,9,128]{1,0,3,2:T(8,128)(2,1)}, u32[]{:S(2)}) copy-start(bf16[8,128,9,128]{1,0,3,2:T(8,128)(2,1)} %copy.74) | copy-start | bytes 7077892
  62.4 9.8 %copy-start.5 = (bf16[1,1,8,128,128]{4,3,2,1,0:T(8,128)(2,1)S(1)}, bf16[1,1,8,128,128]{4,3,2,1,0:T(8,128)(2,1)}, u32[]{:S(2)}) copy-start(bf16[1,1,8,128,128]{4,3,2,1,0:T(8,128)(2,1)} %get-tuple-element.8) | copy-start | bytes 786436
  65.7 10.2 %collective-permute-start.7 = (bf16[1,128,128]{2,1,0:T(8,128)(2,1)}, bf16[1,128,128]{2,1,0:T(8,128)(2,1)}, u32[]{:S(2)}, u32[]{:S(2)}) collective-permute-start(bf16[1,128,128]{2,1,0:T(8,128)(2,1)} %get-tuple-element.15), channel_id=1, source_target_pairs={{1,0},{3,2},{5,4},{7,6},{9,8},{11,10},{13,12},{15,14},{17,16},{19,... | collective-permute-start | bytes 98312 | tf_op jit(solution)/shard_map/ppermute | solution.py:20
  67.0 8.9 %collective-permute-start.6 = (bf16[1,128,128]{2,1,0:T(8,128)(2,1)}, bf16[1,128,128]{2,1,0:T(8,128)(2,1)S(1)}, u32[]{:S(2)}, u32[]{:S(2)}) collective-permute-start(bf16[1,128,128]{2,1,0:T(8,128)(2,1)} %get-tuple-element.14), channel_id=1, source_target_pairs={{0,1},{2,3},{4,5},{6,7},{8,9},{10,11},{12,13},{14,15},{16,17},{18,... | collective-permute-start | bytes 98312 | tf_op jit(solution)/shard_map/ppermute | solution.py:18
  78.1 2.7 %copy-start.4 = (bf16[1,1,8,128,128]{4,3,2,1,0:T(8,128)(2,1)S(1)}, bf16[1,1,8,128,128]{4,3,2,1,0:T(8,128)(2,1)}, u32[]{:S(2)}) copy-start(bf16[1,1,8,128,128]{4,3,2,1,0:T(8,128)(2,1)} %get-tuple-element.6) | copy-start | bytes 786436
  91.1 87.2 %copy-start.11 = (s32[4]{0:T(128)S(1)}, s32[4]{0:T(128)}, u32[]{:S(2)}) copy-start(s32[4]{0:T(128)} %param.11) | copy-start | bytes 52
  91.1 98.5 %copy-start.2 = (bf16[2,72,1152]{2,1,0:T(8,128)(2,1)S(1)}, bf16[2,72,1152]{2,1,0:T(8,128)(2,1)}, u32[]{:S(2)}) copy-start(bf16[2,72,1152]{2,1,0:T(8,128)(2,1)} %param.12) | copy-start | bytes 995332
  91.1 87.2 %all-reduce.6.cloned.1.call-start = ((), (), s32[]{:S(2)}) async-start(), calls=%async_computation.2 | async-start | bytes 147456 | tf_op jit(solution)/shard_map/psum | solution.py:85
  157.3 84.4 %all-gather.2.cloned.1.call-start = ((), (), s32[]{:S(2)}) async-start(), calls=%async_computation.3 | async-start | bytes 1253376 | tf_op jit(solution)/shard_map/all_gather | solution.py:102
  238.4 4.9 %copy-start.8 = (bf16[72,1152]{1,0:T(8,128)(2,1)S(1)}, bf16[72,1152]{1,0:T(8,128)(2,1)}, u32[]{:S(2)}) copy-start(bf16[72,1152]{1,0:T(8,128)(2,1)} %reduce_sum.99) | copy-start | bytes 497668
  238.4 4.9 %copy-start.9 = (bf16[128,128]{1,0:T(8,128)(2,1)S(1)}, bf16[128,128]{1,0:T(8,128)(2,1)}, u32[]{:S(2)}) copy-start(bf16[128,128]{1,0:T(8,128)(2,1)} %reduce_sum.101) | copy-start | bytes 98308
  238.4 4.9 %copy-start.10 = (bf16[128,128]{1,0:T(8,128)(2,1)S(1)}, bf16[128,128]{1,0:T(8,128)(2,1)}, u32[]{:S(2)}) copy-start(bf16[128,128]{1,0:T(8,128)(2,1)} %reduce_sum.100) | copy-start | bytes 98308
Sparse Core Ops, SparseCore 0:
  91.2 64.4 reduce-scatter.1
  158.6 19.6 all-reduce.5
  180.9 38.5 all-gather.1
